TPU v7x, 32 devices: a whole 2x2x4 slice. The times are simulated.
32 devices in a mesh: src: 8 (over y, x, core), tgt: 4 (over z).
Axes of the slice: x: 2, y: 2, z: 4, core: 2. Of those that a mesh axis runs over, the one named last changes fastest.
Arguments:
- src_points: bfloat16 [64, 4096], P(None, ('src', 'tgt')), may hold values from -3 to 3
- tgt_points: bfloat16 [64, 1024], P(None, 'tgt'), may hold values from -3 to 3
- src_log_mass: float32 [4096], P(('src', 'tgt')), may hold values from -4 to 4
- tgt_log_mass: bfloat16 [1024], P('tgt'), may hold values from -4 to 4
- tgt_potential: bfloat16 [1024], P('tgt'), may hold values from -18 to 168
- src_cluster: int32 [4096], P(('src', 'tgt')), may hold values from 0 to 63, as said below
- tgt_cluster: int32 [1024], P('tgt'), may hold values from 0 to 63, as said below
- kept_pairs: int32 [1024, 2], replicated, may hold values from 0 to 63, as said below
Outputs:
- new_src_potential: float32 [4096], P(('src', 'tgt'))
- new_tgt_potential: float32 [1024], P('tgt')
Inputs may be any that keep to these rules, and one draw needn't show every extreme that they name: `src_cluster`: never falls along the cells; every cluster holds at least one cell. `tgt_cluster`: never falls along the cells; every cluster holds at least one cell. `kept_pairs`: each pair stands once; every cluster of either day is in some pair.
All inputs are finite; a program needn't handle non-finite values.
Results may differ from a plain program's by a relative error of at most 0.00045.
Values may be sent and summed in bfloat16 or wider, within the bound.
No kernel may reach another device: no remote copies, remote signals or barrier semaphores. Data moves between devices by JAX's collectives and lax.ppermute only.
A program may use at most 128 MiB of HBM per device.

v0:
```python
import math
import jax
import jax.numpy as jnp
from jax import lax
from jax.sharding import PartitionSpec as P

DIM = 64
CLUSTERS = 64
FLOOR_VALUE = -1e30
EPSILON = 1.0
MASS_FACTOR = 10.0 / 11.0
TILE_WIDTH = 2048


def square_norms(points):
    widened = points.astype(jnp.float32)
    return jnp.sum(widened * widened, axis=0)


def cross_products(left_rows, right_rows):
    return lax.dot_general(
        left_rows, right_rows, (((0,), (0,)), ((), ())), preferred_element_type=jnp.float32
    )


def build_grid(kept_pairs, labels):
    src_side = (kept_pairs[:, 0][:, None] == labels[None, :]).astype(jnp.float32)
    tgt_side = (kept_pairs[:, 1][:, None] == labels[None, :]).astype(jnp.float32)
    return jnp.dot(src_side.T, tgt_side, preferred_element_type=jnp.float32)


def body(
    src_points,
    tgt_points,
    src_log_mass,
    tgt_log_mass,
    tgt_potential,
    src_cluster,
    tgt_cluster,
    kept_pairs,
):
    labels = jnp.arange(CLUSTERS, dtype=jnp.int32)
    pair_grid = build_grid(kept_pairs, labels)
    src_norms = square_norms(src_points)
    src_onehot = (src_cluster[:, None] == labels[None, :]).astype(jnp.float32)
    row_grid = jnp.dot(src_onehot, pair_grid, preferred_element_type=jnp.float32)
    reach = jnp.max(row_grid, axis=0)
    row_table = row_grid.astype(jnp.bfloat16)
    row_count = src_points.shape[1]
    block_width = tgt_points.shape[1]
    side_terms = jnp.stack([tgt_potential, tgt_log_mass, tgt_cluster.astype(jnp.bfloat16)], axis=0)
    packed = jnp.concatenate([tgt_points, side_terms], axis=0)

    def unpack(tile):
        tile_points = tile[:DIM]
        tile_labels = tile[DIM + 2].astype(jnp.int32)
        tgt_onehot = labels[:, None] == tile_labels[None, :]
        has_work = jnp.sum(reach * jnp.max(tgt_onehot.astype(jnp.float32), axis=1)) > 0.5
        return (tile_points, tgt_onehot.astype(jnp.bfloat16), has_work)

    def row_tile(running, tile):
        tile_points, tgt_onehot, has_work = unpack(tile)

        def row_compute(current):
            peak_row, sum_row = current
            kept_mask = jnp.dot(row_table, tgt_onehot, preferred_element_type=jnp.float32) > 0.5
            tile_bias = (
                tile[DIM].astype(jnp.float32) - square_norms(tile_points)
            ) / EPSILON + tile[DIM + 1].astype(jnp.float32)
            scores = (
                tile_bias[None, :]
                - (src_norms[:, None] - 2.0 * cross_products(src_points, tile_points)) / EPSILON
            )
            scores = jnp.where(kept_mask, scores, FLOOR_VALUE)
            new_peak = jnp.maximum(peak_row, jnp.max(scores, axis=1))
            weights = jnp.where(kept_mask, jnp.exp(scores - new_peak[:, None]), 0.0)
            return (new_peak, sum_row * jnp.exp(peak_row - new_peak) + jnp.sum(weights, axis=1))

        return lax.cond(has_work, row_compute, lambda current: current, running)

    start_state = (
        jnp.full((row_count,), FLOOR_VALUE, jnp.float32),
        jnp.zeros((row_count,), jnp.float32),
    )
    targets = lax.all_gather(packed, "tgt", axis=1, tiled=True)
    columns = targets.shape[1]
    tile_width = math.gcd(columns, TILE_WIDTH)

    def advance(number, current):
        return row_tile(
            current, lax.dynamic_slice_in_dim(targets, number * tile_width, tile_width, 1)
        )

    peak_row, sum_row = lax.fori_loop(0, columns // tile_width, advance, start_state)
    new_src = -MASS_FACTOR * EPSILON * (peak_row + jnp.log(sum_row))
    col_bias = (new_src - src_norms) / EPSILON + src_log_mass
    column_targets = lax.all_gather(packed, "tgt", axis=1, tiled=True)
    columns = column_targets.shape[1]
    column_tile_width = math.gcd(columns, TILE_WIDTH)

    def column_tile(number):
        tile = lax.dynamic_slice_in_dim(
            column_targets, number * column_tile_width, column_tile_width, 1
        )
        tile_points, tgt_onehot, has_work = unpack(tile)

        def column_compute(unused):
            kept_mask = jnp.dot(row_table, tgt_onehot, preferred_element_type=jnp.float32) > 0.5
            scores = (
                col_bias[:, None]
                - (
                    square_norms(tile_points)[None, :]
                    - 2.0 * cross_products(src_points, tile_points)
                )
                / EPSILON
            )
            scores = jnp.where(kept_mask, scores, FLOOR_VALUE)
            highest = jnp.max(scores, axis=0)
            weights = jnp.where(kept_mask, jnp.exp(scores - highest[None, :]), 0.0)
            return (highest, jnp.sum(weights, axis=0))

        def skipped(unused):
            return (
                jnp.full((column_tile_width,), FLOOR_VALUE, jnp.float32),
                jnp.zeros((column_tile_width,), jnp.float32),
            )

        return lax.cond(has_work, column_compute, skipped, 0)

    peaks, totals = lax.map(column_tile, jnp.arange(columns // column_tile_width, dtype=jnp.int32))
    piece_peak = peaks.reshape(columns)
    piece_sum = totals.reshape(columns)
    stacked = jnp.stack([piece_peak, piece_sum], axis=0)
    col_peak, col_sum = (stacked[0], stacked[1])
    block_offset = lax.axis_index("tgt") * block_width
    global_peak = lax.pmax(col_peak, ("src", "tgt"))
    rescaled = col_sum * jnp.exp(col_peak - global_peak)
    own_share = lax.psum_scatter(rescaled, "tgt", scatter_dimension=0, tiled=True)
    own_sum = lax.psum(own_share, "src")
    own_peak = lax.dynamic_slice_in_dim(global_peak, block_offset, block_width, 0)
    new_tgt = -MASS_FACTOR * EPSILON * (own_peak + jnp.log(own_sum))
    return (new_src, new_tgt)


def solution(mesh):
    in_specs = (
        P(None, ("src", "tgt")),
        P(None, "tgt"),
        P(("src", "tgt")),
        P("tgt"),
        P("tgt"),
        P(("src", "tgt")),
        P("tgt"),
        P(),
    )
    out_specs = (P(("src", "tgt")), P("tgt"))
    return jax.shard_map(body, mesh=mesh, in_specs=in_specs, out_specs=out_specs, check_vma=False)
```

profile of v0, /device:TPU:0, one launch (start us, length us, event | category | flops | bytes accessed | tf_op | source)
XLA Modules:
  0.0 92.5 jit_solution(2774065129864218746)
XLA Ops:
  0.6 0.7 convert_element_type.50
  1.3 0.0 copy-start.4
  1.3 0.6 copy-done.4
  2.0 0.0 copy-start.5
  2.0 0.6 copy-done.5
  2.6 0.8 pad_maximum_fusion
  3.4 15.2 %all_gather.4 = bf16[67,1024]{1,0:T(8,128)(2,1)S(1)} all-gather(bf16[67,256]{1,0:T(8,128)(2,1)S(1)} %pad_maximum_fusion), channel_id=1, replica_groups=mesh['src'=8,'tgt'=4] {'tgt'}, dimensions={1}, use_global_device_ids=true | all-gather | bytes 171520 | tf_op jit(solution)/shard_map/all_gather | solution.py:85
  18.6 0.0 copy-start.1
  18.6 0.7 copy-done.1
  19.3 0.0 copy-start.6
  19.3 0.6 copy-done.6
  20.0 0.9 fusion.18
  20.8 0.0 copy-start
  20.9 0.7 copy-done
  21.6 0.1 convert_reduce_fusion
  21.7 0.6 multiply_reduce_fusion.3
  23.0 1.0 %conditional.2 = ((f32[128]{0:T(128)S(1)}, f32[128]{0:T(128)S(1)})) conditional(s32[]{:T(128)} %convert_element_type.52, (f32[128]{0:T(128)S(1)}, f32[128]{0:T(128)S(1)}) %tuple.37, (bf16[128,64]{0,1:T(8,128)(2,1)S(1)}, bf16[64,1024]{1,0:T(8,128)(2,1)S(1)}, bf16[67,1024]{1,0:T(8,128)(2,1)S(1)}, bf16[64,1024]{1,0:T(8,128)(2,1)S(1)}, f32[128]{0:T(128)S(1)}, ...), branch_computations={%region_4.5_spmd, %region_5.9_spmd} | conditional | flops 34934016 | bytes 1895448 | solution.py:79
  23.0 0.3 convolution_compare_fusion
  23.3 0.4 fusion.16
  23.7 0.3 select_reduce_fusion
  24.0 0.0 copy-start.3
  24.0 0.0 copy-start.2
  24.0 0.6 copy-done.2
  24.7 0.0 copy-done.3
  24.7 2.0 %conditional.3 = (f32[1024]{0:T(1024)}, f32[1024]{0:T(1024)S(1)}) conditional(s32[]{:T(128)} %convert_element_type.52, () %tuple.39, (bf16[128,64]{0,1:T(8,128)(2,1)S(1)}, bf16[64,1024]{1,0:T(8,128)(2,1)S(1)}, f32[128]{0:T(128)S(1)}, f32[128]{0:T(128)S(1)}, f32[128]{0:T(128)S(1)}, /*index=5*/bf16[64,1024]{1,0:T(8,128)(2,1)S(1)}, ...), branch_computations={%region_9.10_spmd, %region_10.14_spmd} | conditional | flops 34927872 | bytes 1890832 | solution.py:128
  24.7 0.2 convolution_compare_fusion.1
  25.0 0.9 fusion.17
  25.9 0.8 select_reduce_fusion.1
  26.7 40.9 %pmax.7 = f32[1024]{0:T(1024)S(1)} all-reduce(f32[1024]{0:T(1024)} %get-tuple-element.126), channel_id=1, replica_groups=mesh['src'=8,'tgt'=4] {'src','tgt'}, use_global_device_ids=true, to_apply=%region_14.15 | all-reduce | flops 1024 | bytes 8192 | tf_op jit(solution)/shard_map/pmax | solution.py:136
  67.6 0.7 exponential_multiply_fusion
  68.3 9.8 %all-reduce = f32[1024]{0:T(1024)S(1)} all-reduce(f32[1024]{0:T(1024)S(1)} %exponential_multiply_fusion), channel_id=2, replica_groups=mesh['src'=8,'tgt'=4] {'tgt'}, use_global_device_ids=true, to_apply=%region_15.16.clone | all-reduce | flops 1024 | bytes 8192
  78.1 0.0 copy-start.7
  78.1 0.7 copy-done.7
  78.8 0.6 dynamic-slice
  80.0 0.1 dynamic-slice.1
  80.1 11.8 %psum.7 = f32[256]{0:T(256)S(1)} all-reduce(f32[256]{0:T(256)S(1)} %dynamic-slice.1), channel_id=1, replica_groups=mesh['src'=8,'tgt'=4] {'src'}, use_global_device_ids=true, to_apply=%region_16.0 | all-reduce | flops 256 | bytes 2048 | tf_op jit(solution)/shard_map/psum | solution.py:139
  91.9 0.6 add_multiply_fusion
  (18 shorter events, 0.2 us)
Async XLA Ops:
  1.3 0.7 copy-start.4
  2.0 0.7 copy-start.5
  18.6 0.7 copy-start.1
  19.3 0.7 copy-start.6
  20.8 0.7 copy-start
  24.0 0.7 copy-start.3
  24.0 0.7 copy-start.2
  78.1 0.7 copy-start.7
where the time goes:
time: 93.2 us; the launch traced here: 92.5 us
  blocking collectives  77.7 us (83%)
  local copies, waits for them, and re-layouts  5.31 us (6%)
  other arithmetic  4.79 us (5%)
  matrix products  2.63 us (3%)
  between operations  2.03 us (2%)
    pmax x1, blocking collectives, body(): global_peak = lax.pmax(col_peak, ('src', 'tgt'))  40.9 us
    all_gather x1, blocking collectives, body(): targets = lax.all_gather(packed, 'tgt', axis=1, tiled=True)  15.2 us
    psum x1, blocking collectives, body(): own_sum = lax.psum(own_share, 'src')  11.8 us
    unnamed x1, blocking collectives  9.85 us
    unnamed x18, local copies, waits for them, and re-layouts  5.27 us

commit v1 on v0

--- a/solution.py
+++ b/solution.py
@@ -136,7 +136,10 @@
     global_peak = lax.pmax(col_peak, ("src", "tgt"))
     rescaled = col_sum * jnp.exp(col_peak - global_peak)
     own_share = lax.psum_scatter(rescaled, "tgt", scatter_dimension=0, tiled=True)
-    own_sum = lax.psum(own_share, "src")
+    n_dev, own_sum = (lax.axis_size("src"), own_share)
+    for hop in [1 << k for k in range(n_dev.bit_length() - 1)]:
+        swap = [(i, i ^ hop) for i in range(n_dev)]
+        own_sum = own_sum + lax.ppermute(own_sum, "src", swap)
     own_peak = lax.dynamic_slice_in_dim(global_peak, block_offset, block_width, 0)
     new_tgt = -MASS_FACTOR * EPSILON * (own_peak + jnp.log(own_sum))
     return (new_src, new_tgt)

time: 93.2 us -> 89.8 us (0.964)
  blocking collectives: 77.7 us -> 65.9 us
  starting transfers between devices: 0 us -> 4.3 us
  waiting for transfers between devices: 0 us -> 4.26 us
    psum x1 -> x0, blocking collectives: 11.8 us -> none  [body(): own_sum = lax.psum(own_share, 'src')]
    ppermute x0 -> x3, starting transfers between devices: none -> 4.3 us  [body(): own_sum = own_sum + lax.ppermute(own_sum, 'src', swap)]
    ppermute x0 -> x3, waiting for transfers between devices: none -> 4.26 us  [body(): own_sum = own_sum + lax.ppermute(own_sum, 'src', swap)]
  transfers between devices with their start and end apart: 0 -> 3, of which waited for: 0 -> 3; matrix products, arithmetic and copies ran while one was open for 0% -> 0% of each run, Pallas kernels for 0% -> 0%
where the time goes in v1:
time: 89.8 us; the launch traced here: 89.1 us
  blocking collectives  65.9 us (73%)
  local copies, waits for them, and re-layouts  5.03 us (6%)
  other arithmetic  4.87 us (5%)
  starting transfers between devices  4.3 us (5%)
  waiting for transfers between devices  4.26 us (5%)
  matrix products  2.64 us (3%)
  between operations  2.04 us (2%)
    pmax x1, blocking collectives, body(): global_peak = lax.pmax(col_peak, ('src', 'tgt'))  40.8 us
    all_gather x1, blocking collectives, body(): targets = lax.all_gather(packed, 'tgt', axis=1, tiled=True)  15.2 us
    unnamed x1, blocking collectives  9.94 us
    unnamed x18, local copies, waits for them, and re-layouts  4.99 us
    ppermute x3, starting transfers between devices, body(): own_sum = own_sum + lax.ppermute(own_sum, 'src', swap)  4.3 us
    ppermute x3, waiting for transfers between devices, body(): own_sum = own_sum + lax.ppermute(own_sum, 'src', swap)  4.26 us
  transfers between devices with their start and end apart: 3, of which 3 were waited for; matrix products, arithmetic and copies ran while one was open for 0% of the time, Pallas kernels for 0%

profile of v1, /device:TPU:0, one launch (start us, length us, event | category | flops | bytes accessed | tf_op | source)
XLA Modules:
  0.0 89.1 jit_solution(17619792293555911483)
XLA Ops:
  0.6 0.7 convert_element_type.50
  1.3 0.0 copy-start.4
  1.3 0.6 copy-done.4
  2.0 0.0 copy-start.5
  2.0 0.6 copy-done.5
  2.6 0.8 pad_maximum_fusion
  3.4 15.2 %all_gather.4 = bf16[67,1024]{1,0:T(8,128)(2,1)S(1)} all-gather(bf16[67,256]{1,0:T(8,128)(2,1)S(1)} %pad_maximum_fusion), channel_id=1, replica_groups=mesh['src'=8,'tgt'=4] {'tgt'}, dimensions={1}, use_global_device_ids=true | all-gather | bytes 171520 | tf_op jit(solution)/shard_map/all_gather | solution.py:85
  18.6 0.0 copy-start.1
  18.7 0.0 copy-start
  18.7 0.1 convert_reduce_fusion
  18.8 0.5 copy-done.1
  19.3 0.1 copy-done
  19.4 0.0 copy-start.6
  19.4 0.7 copy-done.6
  20.1 0.9 fusion.18
  20.9 0.6 multiply_reduce_fusion.3
  22.2 1.0 %conditional.2 = ((f32[128]{0:T(128)S(1)}, f32[128]{0:T(128)S(1)})) conditional(s32[]{:T(128)} %convert_element_type.52, (f32[128]{0:T(128)S(1)}, f32[128]{0:T(128)S(1)}) %tuple.37, (bf16[128,64]{0,1:T(8,128)(2,1)S(1)}, bf16[64,1024]{1,0:T(8,128)(2,1)S(1)}, bf16[67,1024]{1,0:T(8,128)(2,1)S(1)}, bf16[64,1024]{1,0:T(8,128)(2,1)S(1)}, f32[128]{0:T(128)S(1)}, ...), branch_computations={%region_4.5_spmd, %region_5.9_spmd} | conditional | flops 34934016 | bytes 1895448 | solution.py:79
  22.2 0.2 convolution_compare_fusion
  22.6 0.4 fusion.16
  22.9 0.3 select_reduce_fusion
  23.2 0.0 copy-start.2
  23.3 0.6 copy-done.2
  23.9 0.0 copy-start.3
  23.9 0.5 copy-done.3
  24.4 2.0 %conditional.3 = (f32[1024]{0:T(1024)}, f32[1024]{0:T(1024)S(1)}) conditional(s32[]{:T(128)} %convert_element_type.52, () %tuple.39, (bf16[128,64]{0,1:T(8,128)(2,1)S(1)}, bf16[64,1024]{1,0:T(8,128)(2,1)S(1)}, f32[128]{0:T(128)S(1)}, f32[128]{0:T(128)S(1)}, f32[128]{0:T(128)S(1)}, /*index=5*/bf16[64,1024]{1,0:T(8,128)(2,1)S(1)}, ...), branch_computations={%region_9.10_spmd, %region_10.14_spmd} | conditional | flops 34927872 | bytes 1890832 | solution.py:128
  24.4 0.3 convolution_compare_fusion.1
  24.7 0.9 %fusion.17 = (f32[1024]{0:T(1024)}, f32[128,1024]{1,0:T(8,128)S(1)}) fusion(pred[128,1024]{1,0:T(32,128)(4,1)S(1)} %convolution_compare_fusion.1, bf16[64,128]{1,0:T(8,128)(2,1)S(1)} %get-tuple-element.117, bf16[64,1024]{1,0:T(8,128)(2,1)S(1)} %get-tuple-element.116, f32[1024]{0:T(1024)S(1)} %multiply_reduce_fusion.1, f32[128]{0:T(128)S(1)} %subtract_add_fusion), kind=kOutput, calls=%fused_computation.37 | convolution fusion | flops 17431552 | bytes 811520 | tf_op jit(solution)/shard_map/while/body/eval_jaxpr/cond/branch_1_fun/dot_general | solution.py:21
  25.6 0.8 select_reduce_fusion.1
  26.5 40.8 %pmax.7 = f32[1024]{0:T(1024)S(1)} all-reduce(f32[1024]{0:T(1024)} %get-tuple-element.126), channel_id=1, replica_groups=mesh['src'=8,'tgt'=4] {'src','tgt'}, use_global_device_ids=true, to_apply=%region_14.15 | all-reduce | flops 1024 | bytes 8192 | tf_op jit(solution)/shard_map/pmax | solution.py:136
  67.3 0.7 exponential_multiply_fusion
  67.9 9.9 %all-reduce = f32[1024]{0:T(1024)S(1)} all-reduce(f32[1024]{0:T(1024)S(1)} %exponential_multiply_fusion), channel_id=2, replica_groups=mesh['src'=8,'tgt'=4] {'tgt'}, use_global_device_ids=true, to_apply=%region_15.16.clone | all-reduce | flops 1024 | bytes 8192
  77.9 0.0 copy-start.7
  77.9 0.6 copy-done.7
  78.5 0.6 dynamic-slice
  79.8 0.1 dynamic-slice.1
  79.8 0.0 collective-permute-start
  79.9 1.1 %collective-permute-done = f32[256]{0:T(256)S(1)} collective-permute-done((f32[256]{0:T(256)S(1)}, f32[256]{0:T(256)S(1)}, u32[]{:S(2)}, u32[]{:S(2)}) %collective-permute-start) | collective-permute-done | bytes 1056 | tf_op jit(solution)/shard_map/ppermute | solution.py:142
  81.0 0.1 dynamic-slice_add_fusion
  81.1 2.3 %collective-permute-start.1 = (f32[256]{0:T(256)S(1)}, f32[256]{0:T(256)S(1)}, u32[]{:S(2)}, u32[]{:S(2)}) collective-permute-start(f32[256]{0:T(256)S(1)} %dynamic-slice_add_fusion), channel_id=1, source_target_pairs={{0,8},{4,12},{8,0},{12,4},{16,24},{20,28},{24,16},{28,20},{1,9},{5... | collective-permute-start | bytes 3080 | tf_op jit(solution)/shard_map/ppermute | solution.py:142
  83.4 1.6 %collective-permute-done.1 = f32[256]{0:T(256)S(1)} collective-permute-done((f32[256]{0:T(256)S(1)}, f32[256]{0:T(256)S(1)}, u32[]{:S(2)}, u32[]{:S(2)}) %collective-permute-start.1) | collective-permute-done | bytes 1056 | tf_op jit(solution)/shard_map/ppermute | solution.py:142
  84.9 2.0 %collective-permute-start.2 = (f32[256]{0:T(256)S(1)}, f32[256]{0:T(256)S(1)}, u32[]{:S(2)}, u32[]{:S(2)}) collective-permute-start(f32[256]{0:T(256)S(1)} %add.44), channel_id=1, source_target_pairs={{0,16},{4,20},{8,24},{12,28},{16,0},{20,4},{24,8},{28,12},{1,17},{... | collective-permute-start | bytes 3080 | tf_op jit(solution)/shard_map/ppermute | solution.py:142
  86.9 1.6 %collective-permute-done.2 = f32[256]{0:T(256)S(1)} collective-permute-done((f32[256]{0:T(256)S(1)}, f32[256]{0:T(256)S(1)}, u32[]{:S(2)}, u32[]{:S(2)}) %collective-permute-start.2) | collective-permute-done | bytes 1056 | tf_op jit(solution)/shard_map/ppermute | solution.py:142
  88.5 0.6 add_multiply_fusion
  (19 shorter events, 0.2 us)
Async XLA Ops:
  1.3 0.7 copy-start.4
  2.0 0.7 copy-start.5
  18.6 0.7 copy-start.1
  18.7 0.7 copy-start
  19.4 0.7 copy-start.6
  23.2 0.7 copy-start.2
  23.9 0.5 copy-start.3
  77.9 0.7 copy-start.7
  79.8 1.2 %collective-permute-start = (f32[256]{0:T(256)S(1)}, f32[256]{0:T(256)S(1)}, u32[]{:S(2)}, u32[]{:S(2)}) collective-permute-start(f32[256]{0:T(256)S(1)} %dynamic-slice.1), channel_id=1, source_target_pairs={{0,4},{4,0},{8,12},{12,8},{16,20},{20,16},{24,28},{28,24},{1,5},{5... | collective-permute-start | bytes 3080 | tf_op jit(solution)/shard_map/ppermute | solution.py:142
  81.1 3.8 %collective-permute-start.1 = (f32[256]{0:T(256)S(1)}, f32[256]{0:T(256)S(1)}, u32[]{:S(2)}, u32[]{:S(2)}) collective-permute-start(f32[256]{0:T(256)S(1)} %dynamic-slice_add_fusion), channel_id=1, source_target_pairs={{0,8},{4,12},{8,0},{12,4},{16,24},{20,28},{24,16},{28,20},{1,9},{5... | collective-permute-start | bytes 3080 | tf_op jit(solution)/shard_map/ppermute | solution.py:142
  84.9 3.6 %collective-permute-start.2 = (f32[256]{0:T(256)S(1)}, f32[256]{0:T(256)S(1)}, u32[]{:S(2)}, u32[]{:S(2)}) collective-permute-start(f32[256]{0:T(256)S(1)} %add.44), channel_id=1, source_target_pairs={{0,16},{4,20},{8,24},{12,28},{16,0},{20,4},{24,8},{28,12},{1,17},{... | collective-permute-start | bytes 3080 | tf_op jit(solution)/shard_map/ppermute | solution.py:142
